TPU v7x, 256 devices: a whole 4x4x8 slice. The times are simulated.
256 devices in a mesh: dp: 64 (over x, z, core), rep: 4 (over y).
Axes of the slice: x: 4, y: 4, z: 8, core: 2. Of those that a mesh axis runs over, the one named last changes fastest.
Arguments:
- frames_in: bfloat16 [4, 57344, 1536], P('rep', 'dp')
- lengths: int32 [4, 64, 4], P('rep', 'dp'), may hold values from 1 to 893, as said below
- norm_gain: float32 [1536], replicated, may hold values from 0.5 to 1.5
- norm_bias: float32 [1536], replicated, may hold values from -2 to 2
- w_in: bfloat16 [1536, 3072], P(('dp', 'rep')), may hold values from -0.15625 to 0.15625
- kernel: float32 [31, 1536], replicated, may hold values from -1 to 1
- batch_gain: float32 [1536], replicated, may hold values from 0.5 to 1.5
- batch_bias: float32 [1536], replicated, may hold values from -3 to 3
- w_out: bfloat16 [1536, 1536], P(('dp', 'rep')), may hold values from -0.15625 to 0.15625
Outputs:
- frames_out: bfloat16 [4, 57344, 1536], P('rep', 'dp')
Inputs may be any that keep to these rules, and one draw needn't show every extreme that they name: `lengths`: for each rep index, the devices 2k and 2k + 1 of dp hold 1024 frames together, so each rep index holds 512 frames for each of its dp devices; a device holds at most 896 frames, and some device of every rep index holds exactly 896.
All inputs are finite; a program needn't handle non-finite values.
Results may differ from a plain program's by a relative error of at most 0.0038.
Values may be sent and summed in bfloat16 or wider, within the bound.
A program may use at most 128 MiB of HBM per device.

v0:
```python
import jax
import jax.numpy as jnp
from jax import lax
from jax.sharding import PartitionSpec as P

FR_DEV = 512
EPSILON = 1e-05


def layer_norm(frames, norm_gain, norm_bias):
    values = frames.astype(jnp.float32)
    average = jnp.mean(values, axis=-1, keepdims=True)
    centred = values - average
    spread = jnp.mean(centred * centred, axis=-1, keepdims=True)
    return centred * lax.rsqrt(spread + EPSILON) * norm_gain + norm_bias


def depthwise(gated, labels, kernel):
    half_kernel = kernel.shape[0] // 2
    length_rows = gated.shape[0]
    padded = jnp.pad(gated, ((half_kernel, half_kernel), (0, 0)))
    padded_labels = jnp.pad(labels, (half_kernel, half_kernel), constant_values=-1)
    summed = jnp.zeros(gated.shape, jnp.float32)
    for offset in range(kernel.shape[0]):
        shared = padded_labels[offset : offset + length_rows] == labels
        contribution = jnp.where(
            shared[:, None], padded[offset : offset + length_rows].astype(jnp.float32), 0.0
        )
        summed = summed + contribution * kernel[offset]
    return summed


def project_in(normed, weight_rows):
    return jnp.dot(normed, weight_rows, preferred_element_type=jnp.float32)


def project_out(active, weight_rows):
    return jnp.dot(active, weight_rows, preferred_element_type=jnp.float32)


def on_device(
    frames_in, lengths, norm_gain, norm_bias, w_in, kernel, batch_gain, batch_bias, w_out
):
    local_frames = frames_in[0]
    local_lengths = lengths[0, 0]
    capacity = local_frames.shape[0]
    features = local_frames.shape[1]
    total_count = lax.axis_size("dp") * lax.axis_size("rep") * FR_DEV
    grouped = (w_in, w_out)
    grouped = (
        lax.all_gather(w_in, ("dp", "rep"), axis=0, tiled=True),
        lax.all_gather(w_out, ("dp", "rep"), axis=0, tiled=True),
    )
    rows_here = jnp.arange(capacity, dtype=jnp.int32)
    local_load = jnp.sum(local_lengths)
    bounds = jnp.cumsum(local_lengths)
    labels = jnp.sum((rows_here[:, None] >= bounds[None, :]).astype(jnp.int32), axis=1)
    row_weight = (rows_here < local_load).astype(jnp.float32)[:, None]
    normed = layer_norm(local_frames, norm_gain, norm_bias).astype(jnp.bfloat16)
    projected = project_in(normed, grouped[0])
    gated = (projected[:, :features] * jax.nn.sigmoid(projected[:, features:])).astype(jnp.bfloat16)
    convolved = depthwise(gated, labels, kernel)
    average = lax.psum(jnp.sum(convolved * row_weight, axis=0), ("dp", "rep")) / total_count
    centred = convolved - average
    spread = lax.psum(jnp.sum(centred * centred * row_weight, axis=0), ("dp", "rep")) / total_count
    scaled = centred * lax.rsqrt(spread + EPSILON) * batch_gain + batch_bias
    active = jax.nn.silu(scaled).astype(jnp.bfloat16)
    branch = project_out(active, grouped[1])
    mixed = (local_frames.astype(jnp.float32) + branch).astype(jnp.bfloat16)
    result = jnp.where(rows_here[:, None] < local_load, mixed, jnp.zeros_like(mixed))
    return result[None]


def solution(mesh):
    placed = (
        P("rep", "dp", None),
        P("rep", "dp", None),
        P(),
        P(),
        P(("dp", "rep"), None),
        P(),
        P(),
        P(),
        P(("dp", "rep"), None),
    )
    return jax.shard_map(
        on_device, mesh=mesh, in_specs=placed, out_specs=P("rep", "dp", None), check_vma=False
    )
```

profile of v0, /device:TPU:1, one launch (start us, length us, event | category | flops | bytes accessed | tf_op | source)
XLA Modules:
  0.0 487.7 jit_solution(4124133330554323458)
XLA Ops:
  6.5 0.0 all-gather.7.cloned.1.call-start
  6.5 0.7 all-gather.7.cloned.1.call-update
  7.3 0.0 all-gather.5.cloned.1.call-start
  7.3 0.7 all-gather.5.cloned.1.call-update
  8.0 1.3 reduce_sum.54
  9.3 0.8 reduce-window.8
  10.1 0.6 iota_compare_fusion.1
  10.8 0.7 fusion.26
  11.4 0.1 convert_reduce_fusion.1
  11.5 1.5 slice_reduce_fusion.29
  13.0 1.8 slice_reduce_fusion.30
  14.9 0.1 slice_compare_fusion.26
  14.9 2.2 convert_reduce_fusion
  17.2 2.6 fusion.4
  19.8 0.1 slice_compare_fusion.29
  19.9 0.1 slice_compare_fusion.28
  20.0 0.1 slice_compare_fusion.27
  20.1 111.2 %all-gather.7.cloned.1.call-done = bf16[256,6,1536]{2,1,0:T(8,128)(2,1)} async-done(((bf16[1,6,1536]{2,1,0:T(8,128)(2,1)}), bf16[256,6,1536]{2,1,0:T(8,128)(2,1)}) %all-gather.7.cloned.1.call-update) | async-done | bytes 4718608 | tf_op jit(solution)/shard_map/all_gather | solution.py:52
  131.3 8.5 %reshape.87 = bf16[1536,1536]{1,0:T(8,128)(2,1)} reshape(bf16[256,6,1536]{2,1,0:T(8,128)(2,1)} %all-gather.7.cloned.1.call-done) | data formatting | bytes 9437184
  139.8 0.0 copy-start
  139.8 0.0 copy-start.2
  139.8 0.0 copy-start.3
  139.8 113.5 %all-gather.5.cloned.1.call-done = bf16[256,6,3072]{2,1,0:T(8,128)(2,1)} async-done(((bf16[1,6,3072]{2,1,0:T(8,128)(2,1)}), bf16[256,6,3072]{2,1,0:T(8,128)(2,1)}) %all-gather.5.cloned.1.call-update) | async-done | bytes 9437200 | tf_op jit(solution)/shard_map/all_gather | solution.py:51
  253.3 14.2 %reshape.85 = bf16[1536,3072]{1,0:T(8,128)(2,1)} reshape(bf16[256,6,3072]{2,1,0:T(8,128)(2,1)} %all-gather.5.cloned.1.call-done) | data formatting | bytes 18874368
  267.5 0.0 copy-done
  267.5 0.0 copy-done.2
  267.5 0.0 copy-done.3
  267.5 11.3 %fusion.16 = f32[896,3072]{1,0:T(8,128)S(1)} fusion(bf16[1536,3072]{1,0:T(8,128)(2,1)} %reshape.85, bf16[1,896,1536]{2,1,0:T(8,128)(2,1)S(1)} %copy-done, f32[1536]{0:T(1024)S(1)} %copy-done.2, f32[1536]{0:T(1024)S(1)} %copy-done.3, f32[896]{0:T(1024)S(1)} %add_rsqrt_fusion.1, f32[896]{0:T(1024)S(1)} %broadcast_multiply_fusion.1), kind=kOutput, calls=%fused_computation.23 | convolution fusion | flops 8463974400 | bytes 23219200 | tf_op jit(solution)/shard_map/dot_general | solution.py:34
  278.8 1.5 fusion.13
  280.4 0.0 copy-start.4
  280.4 0.0 copy-start.5
  280.4 38.3 %multiply_reduce_fusion.1 = (f32[1536]{0:T(1024)S(1)}, f32[896,1536]{1,0:T(8,128)}) fusion(f32[896]{0:T(1024)S(1)} %fusion.26, f32[1536]{0:T(1024)S(1)} %get-tuple-element.34, pred[896]{0:T(1024)(128)(4,1)S(1)} %get-tuple-element.67, f32[1536]{0:T(1024)S(1)} %get-tuple-element.35, pred[896]{0:T(1024)(128)(4,1)S(1)} %get-tuple-element.39, ...), kind=kLoop, calls=%fused_computation.18 | loop fusion | flops 170654208 | bytes 8484608 | tf_op jit(solution)/shard_map/reduce_sum | solution.py:63
  318.7 0.0 copy-start.1
  318.7 74.8 %psum.14 = f32[1536]{0:T(1024)S(1)} all-reduce(f32[1536]{0:T(1024)S(1)} %get-tuple-element.36), channel_id=1, replica_groups=mesh['dp'=64,'rep'=4] {'dp','rep'}, use_global_device_ids=true, to_apply=%region_6.7 | all-reduce | flops 1536 | bytes 12288 | tf_op jit(solution)/shard_map/psum | solution.py:63
  393.5 3.3 multiply_reduce_fusion
  396.8 73.6 %psum.15 = f32[1536]{0:T(1024)S(1)} all-reduce(f32[1536]{0:T(1024)S(1)} %multiply_reduce_fusion), channel_id=1, replica_groups=mesh['dp'=64,'rep'=4] {'dp','rep'}, use_global_device_ids=true, to_apply=%region_8.9 | all-reduce | flops 1536 | bytes 12288 | tf_op jit(solution)/shard_map/psum | solution.py:65
  470.4 0.0 copy-done.4
  470.4 0.0 copy-done.5
  470.4 0.0 copy-done.1
  470.4 10.4 %fusion.15 = bf16[1,896,1536]{2,1,0:T(8,128)(2,1)} fusion(bf16[1536,1536]{1,0:T(8,128)(2,1)} %reshape.87, bf16[1,896,1536]{2,1,0:T(8,128)(2,1)S(1)} %copy-done.1, f32[896,1536]{1,0:T(8,128)} %get-tuple-element.37, f32[1536]{0:T(1024)S(1)} %copy-done.4, f32[1536]{0:T(1024)S(1)} %copy-done.5, f32[1536]{0:T(1024)S(1)} %add_rsqrt_fusion, ...), kind=kOutput, calls=%fused_computation.22 | convolution fusion | flops 4245749760 | bytes 15754112 | tf_op jit(solution)/shard_map/dot_general | solution.py:38
  (4 shorter events, 0.0 us)
Async XLA Ops:
  6.5 124.8 %all-gather.7.cloned.1.call-start = ((), (), s32[]{:S(2)}) async-start(), calls=%async_computation.1 | async-start | bytes 6316032 | tf_op jit(solution)/shard_map/all_gather | solution.py:52
  7.3 246.1 %all-gather.5.cloned.1.call-start = ((), (), s32[]{:S(2)}) async-start(), calls=%async_computation | async-start | bytes 12632064 | tf_op jit(solution)/shard_map/all_gather | solution.py:51
  139.8 127.7 %copy-start = (bf16[1,896,1536]{2,1,0:T(8,128)(2,1)S(1)}, bf16[1,896,1536]{2,1,0:T(8,128)(2,1)}, u32[]{:S(2)}) copy-start(bf16[1,896,1536]{2,1,0:T(8,128)(2,1)} %param.9) | copy-start | bytes 8257540
  139.8 127.7 %copy-start.2 = (f32[1536]{0:T(1024)S(1)}, f32[1536]{0:T(1024)}, u32[]{:S(2)}) copy-start(f32[1536]{0:T(1024)} %param.12) | copy-start | bytes 18436
  139.8 127.7 %copy-start.3 = (f32[1536]{0:T(1024)S(1)}, f32[1536]{0:T(1024)}, u32[]{:S(2)}) copy-start(f32[1536]{0:T(1024)} %param.11) | copy-start | bytes 18436
  280.4 190.1 %copy-start.4 = (f32[1536]{0:T(1024)S(1)}, f32[1536]{0:T(1024)}, u32[]{:S(2)}) copy-start(f32[1536]{0:T(1024)} %param.16) | copy-start | bytes 18436
  280.4 190.1 %copy-start.5 = (f32[1536]{0:T(1024)S(1)}, f32[1536]{0:T(1024)}, u32[]{:S(2)}) copy-start(f32[1536]{0:T(1024)} %param.15) | copy-start | bytes 18436
  318.7 151.7 %copy-start.1 = (bf16[1,896,1536]{2,1,0:T(8,128)(2,1)S(1)}, bf16[1,896,1536]{2,1,0:T(8,128)(2,1)}, u32[]{:S(2)}) copy-start(bf16[1,896,1536]{2,1,0:T(8,128)(2,1)} %param.9) | copy-start | bytes 8257540
Sparse Core Ops, SparseCore 0:
  11.2 120.0 all-gather.6
  135.1 118.1 all-gather.4
where the time goes:
time: 489 us; the launch traced here: 488 us
  waiting for transfers between devices  226 us (46%)
  blocking collectives  148 us (30%)
  other arithmetic  51.8 us (11%)
  local copies, waits for them, and re-layouts  26 us (5%)
  matrix products  21.8 us (4%)
  between operations  13.5 us (3%)
    all_gather x1, waiting for transfers between devices, on_device(): lax.all_gather(w_in, ('dp', 'rep'), axis=0, tiled=True)  114 us
    all_gather x1, waiting for transfers between devices, on_device(): lax.all_gather(w_out, ('dp', 'rep'), axis=0, tiled=True)  111 us
    psum x1, blocking collectives, on_device(): lax.psum(jnp.sum(convolved * row_weight, axis=0), ('dp', 'rep'))  74.8 us
    psum x1, blocking collectives, on_device(): lax.psum(jnp.sum(centred * centred * row_weight, axis=0), ('dp', 'rep'))  73.6 us
    reduce_sum x1, other arithmetic, on_device(): jnp.sum(convolved * row_weight, axis=0)  38.3 us
    unnamed x14, local copies, waits for them, and re-layouts  22.6 us
    dot_general x1, matrix products, project_in(): return jnp.dot(normed, weight_rows, preferred_element_type=jnp.float32)  11.3 us
    dot_general x1, matrix products, project_out(): return jnp.dot(active, weight_rows, preferred_element_type=jnp.float32)  10.4 us
  transfers between devices with their start and end apart: 2, of which 2 were waited for; matrix products, arithmetic and copies ran while one was open for 4% of the time, Pallas kernels for 0%

commit v1 on v0

--- a/solution.py
+++ b/solution.py
@@ -60,7 +60,10 @@
     projected = project_in(normed, grouped[0])
     gated = (projected[:, :features] * jax.nn.sigmoid(projected[:, features:])).astype(jnp.bfloat16)
     convolved = depthwise(gated, labels, kernel)
-    average = lax.psum(jnp.sum(convolved * row_weight, axis=0), ("dp", "rep")) / total_count
+    average = (
+        jnp.sum(lax.all_gather(jnp.sum(convolved * row_weight, axis=0), ("dp", "rep")), axis=0)
+        / total_count
+    )
     centred = convolved - average
     spread = lax.psum(jnp.sum(centred * centred * row_weight, axis=0), ("dp", "rep")) / total_count
     scaled = centred * lax.rsqrt(spread + EPSILON) * batch_gain + batch_bias

time: 489 us -> 458 us (0.937)
  blocking collectives: 148 us -> 77.1 us
  waiting for transfers between devices: 226 us -> 264 us
    all_gather x0 -> x1, waiting for transfers between devices: none -> 95.6 us  [on_device(): lax.all_gather(jnp.sum(convolved * row_weight, axis=0), ('dp', 'rep'))]
    psum x1 -> x0, blocking collectives: 74.8 us -> none  [on_device(): lax.psum(jnp.sum(convolved * row_weight, axis=0), ('dp', 'rep'))]
    all_gather x1, waiting for transfers between devices: 111 us -> 50.2 us  [on_device(): lax.all_gather(w_out, ('dp', 'rep'), axis=0, tiled=True)]
    unnamed x14 -> x17, local copies, waits for them, and re-layouts: 22.6 us -> 23.2 us
  transfers between devices with their start and end apart: 2 -> 3, of which waited for: 2 -> 3; matrix products, arithmetic and copies ran while one was open for 4% -> 19% of each run, Pallas kernels for 0% -> 0%
where the time goes in v1:
time: 458 us; the launch traced here: 457 us
  waiting for transfers between devices  264 us (58%)
  blocking collectives  77.1 us (17%)
  other arithmetic  53.6 us (12%)
  local copies, waits for them, and re-layouts  26.6 us (6%)
  matrix products  21.8 us (5%)
  between operations  13.2 us (3%)
    all_gather x1, waiting for transfers between devices, on_device(): lax.all_gather(w_in, ('dp', 'rep'), axis=0, tiled=True)  117 us
    all_gather x1, waiting for transfers between devices, on_device(): lax.all_gather(jnp.sum(convolved * row_weight, axis=0), ('dp', 'rep'))  95.6 us
    psum x1, blocking collectives, on_device(): lax.psum(jnp.sum(centred * centred * row_weight, axis=0), ('dp', 'rep'))  77.1 us
    all_gather x1, waiting for transfers between devices, on_device(): lax.all_gather(w_out, ('dp', 'rep'), axis=0, tiled=True)  50.2 us
    reduce_sum x1, other arithmetic, on_device(): jnp.sum(convolved * row_weight, axis=0)  38.3 us
    unnamed x17, local copies, waits for them, and re-layouts  23.2 us
    dot_general x1, matrix products, project_in(): return jnp.dot(normed, weight_rows, preferred_element_type=jnp.float32)  11.3 us
    dot_general x1, matrix products, project_out(): return jnp.dot(active, weight_rows, preferred_element_type=jnp.float32)  10.5 us
  transfers between devices with their start and end apart: 3, of which 3 were waited for; matrix products, arithmetic and copies ran while one was open for 19% of the time, Pallas kernels for 0%

profile of v1, /device:TPU:1, one launch (start us, length us, event | category | flops | bytes accessed | tf_op | source)
XLA Modules:
  0.0 456.7 jit_solution(2228662240689349698)
XLA Ops:
  6.5 0.0 copy-start.6
  6.5 0.0 all-gather.8.cloned.1.call-start
  6.5 0.7 all-gather.8.cloned.1.call-update
  7.3 0.0 all-gather.12.cloned.1.call-start
  7.3 0.7 all-gather.12.cloned.1.call-update
  8.0 0.0 all-gather.10.cloned.1.call-start
  8.1 1.9 slice_reduce_fusion.30
  9.9 0.8 reduce-window.8
  10.7 0.1 convert_reduce_fusion.1
  10.8 0.1 slice_compare_fusion.26
  10.9 2.2 convert_reduce_fusion
  13.1 2.6 fusion.4
  15.8 1.6 slice_reduce_fusion.29
  17.3 0.0 copy-done.6
  17.3 0.7 reduce_sum.63
  18.0 0.7 fusion.26
  18.7 0.1 slice_compare_fusion.29
  18.8 0.1 slice_compare_fusion.28
  18.9 0.1 slice_compare_fusion.27
  19.0 0.0 copy-start
  19.0 0.0 copy-start.2
  19.0 0.0 copy-start.3
  19.0 117.1 %all-gather.8.cloned.1.call-done = bf16[256,6,3072]{2,1,0:T(8,128)(2,1)} async-done(((bf16[1,6,3072]{2,1,0:T(8,128)(2,1)}), bf16[256,6,3072]{2,1,0:T(8,128)(2,1)}) %all-gather.8.cloned.1.call-update) | async-done | bytes 9437200 | tf_op jit(solution)/shard_map/all_gather | solution.py:51
  136.1 14.2 %reshape.88 = bf16[1536,3072]{1,0:T(8,128)(2,1)} reshape(bf16[256,6,3072]{2,1,0:T(8,128)(2,1)} %all-gather.8.cloned.1.call-done) | data formatting | bytes 18874368
  150.2 0.0 copy-done
  150.3 0.0 copy-done.2
  150.3 0.0 copy-done.3
  150.3 11.3 %fusion.16 = f32[896,3072]{1,0:T(8,128)S(1)} fusion(bf16[1536,3072]{1,0:T(8,128)(2,1)} %reshape.88, bf16[1,896,1536]{2,1,0:T(8,128)(2,1)S(1)} %copy-done, f32[1536]{0:T(1024)S(1)} %copy-done.2, f32[1536]{0:T(1024)S(1)} %copy-done.3, f32[896]{0:T(1024)S(1)} %add_rsqrt_fusion.1, f32[896]{0:T(1024)S(1)} %broadcast_multiply_fusion.1), kind=kOutput, calls=%fused_computation.23 | convolution fusion | flops 8463974400 | bytes 23219200 | tf_op jit(solution)/shard_map/dot_general | solution.py:34
  161.6 1.5 fusion.13
  163.1 38.3 %multiply_reduce_fusion.1 = (f32[1536]{0:T(1024)S(1)}, f32[896,1536]{1,0:T(8,128)}) fusion(f32[896]{0:T(1024)S(1)} %fusion.26, f32[1536]{0:T(1024)S(1)} %get-tuple-element.34, pred[896]{0:T(1024)(128)(4,1)S(1)} %get-tuple-element.67, f32[1536]{0:T(1024)S(1)} %get-tuple-element.35, pred[896]{0:T(1024)(128)(4,1)S(1)} %get-tuple-element.39, ...), kind=kLoop, calls=%fused_computation.18 | loop fusion | flops 170654208 | bytes 8484608 | tf_op jit(solution)/shard_map/reduce_sum | solution.py:64
  201.5 0.6 reshape.89
  202.1 0.0 all-gather.10.cloned.1.call-update
  202.1 0.7 iota_compare_fusion.1
  202.8 50.2 %all-gather.12.cloned.1.call-done = bf16[256,6,1536]{2,1,0:T(8,128)(2,1)} async-done(((bf16[1,6,1536]{2,1,0:T(8,128)(2,1)}), bf16[256,6,1536]{2,1,0:T(8,128)(2,1)}) %all-gather.12.cloned.1.call-update) | async-done | bytes 4718608 | tf_op jit(solution)/shard_map/all_gather | solution.py:52
  253.0 8.4 %reshape.92 = bf16[1536,1536]{1,0:T(8,128)(2,1)} reshape(bf16[256,6,1536]{2,1,0:T(8,128)(2,1)} %all-gather.12.cloned.1.call-done) | data formatting | bytes 9437184
  261.4 0.0 copy-start.1
  261.4 0.0 copy-start.4
  261.4 0.0 copy-start.5
  261.4 95.6 %all-gather.10.cloned.1.call-done = f32[256,1,1536]{2,1,0:T(1,128)} async-done(((f32[1,1,1536]{2,1,0:T(1,128)}), f32[256,1,1536]{2,1,0:T(1,128)}) %all-gather.10.cloned.1.call-update) | async-done | bytes 1572880 | tf_op jit(solution)/shard_map/all_gather | solution.py:64
  357.0 2.3 reduce_sum.68
  359.3 3.3 multiply_reduce_fusion
  362.6 77.1 %psum.7 = f32[1536]{0:T(1024)S(1)} all-reduce(f32[1536]{0:T(1024)S(1)} %multiply_reduce_fusion), channel_id=1, replica_groups=mesh['dp'=64,'rep'=4] {'dp','rep'}, use_global_device_ids=true, to_apply=%region_8.9 | all-reduce | flops 1536 | bytes 12288 | tf_op jit(solution)/shard_map/psum | solution.py:68
  439.7 0.0 copy-done.1
  439.7 0.0 copy-done.4
  439.7 0.0 copy-done.5
  439.7 10.5 %fusion.15 = bf16[1,896,1536]{2,1,0:T(8,128)(2,1)} fusion(bf16[1536,1536]{1,0:T(8,128)(2,1)} %reshape.92, bf16[1,896,1536]{2,1,0:T(8,128)(2,1)S(1)} %copy-done.1, f32[896,1536]{1,0:T(8,128)} %get-tuple-element.37, f32[1536]{0:T(1024)S(1)} %copy-done.4, f32[1536]{0:T(1024)S(1)} %copy-done.5, f32[1536]{0:T(1024)S(1)} %add_rsqrt_fusion, ...), kind=kOutput, calls=%fused_computation.22 | convolution fusion | flops 4245749760 | bytes 15754112 | tf_op jit(solution)/shard_map/dot_general | solution.py:38
  (4 shorter events, 0.0 us)
Async XLA Ops:
  6.5 10.8 %copy-start.6 = (s32[1,1,4]{2,1,0:T(1,128)S(1)}, s32[1,1,4]{2,1,0:T(1,128)}, u32[]{:S(2)}) copy-start(s32[1,1,4]{2,1,0:T(1,128)} %param.10) | copy-start | bytes 52
  6.5 129.5 %all-gather.8.cloned.1.call-start = ((), (), s32[]{:S(2)}) async-start(), calls=%async_computation | async-start | bytes 12632064 | tf_op jit(solution)/shard_map/all_gather | solution.py:51
  7.3 245.7 %all-gather.12.cloned.1.call-start = ((), (), s32[]{:S(2)}) async-start(), calls=%async_computation.2 | async-start | bytes 6316032 | tf_op jit(solution)/shard_map/all_gather | solution.py:52
  8.0 349.0 %all-gather.10.cloned.1.call-start = ((), (), s32[]{:S(2)}) async-start(), calls=%async_computation.1 | async-start | bytes 1579008 | tf_op jit(solution)/shard_map/all_gather | solution.py:64
  19.0 131.3 %copy-start = (bf16[1,896,1536]{2,1,0:T(8,128)(2,1)S(1)}, bf16[1,896,1536]{2,1,0:T(8,128)(2,1)}, u32[]{:S(2)}) copy-start(bf16[1,896,1536]{2,1,0:T(8,128)(2,1)} %param.9) | copy-start | bytes 8257540
  19.0 131.3 %copy-start.2 = (f32[1536]{0:T(1024)S(1)}, f32[1536]{0:T(1024)}, u32[]{:S(2)}) copy-start(f32[1536]{0:T(1024)} %param.12) | copy-start | bytes 18436
  19.0 131.2 %copy-start.3 = (f32[1536]{0:T(1024)S(1)}, f32[1536]{0:T(1024)}, u32[]{:S(2)}) copy-start(f32[1536]{0:T(1024)} %param.11) | copy-start | bytes 18436
  261.4 178.3 %copy-start.1 = (bf16[1,896,1536]{2,1,0:T(8,128)(2,1)S(1)}, bf16[1,896,1536]{2,1,0:T(8,128)(2,1)}, u32[]{:S(2)}) copy-start(bf16[1,896,1536]{2,1,0:T(8,128)(2,1)} %param.9) | copy-start | bytes 8257540
  261.4 178.3 %copy-start.4 = (f32[1536]{0:T(1024)S(1)}, f32[1536]{0:T(1024)}, u32[]{:S(2)}) copy-start(f32[1536]{0:T(1024)} %param.16) | copy-start | bytes 18436
  261.4 178.3 %copy-start.5 = (f32[1536]{0:T(1024)S(1)}, f32[1536]{0:T(1024)}, u32[]{:S(2)}) copy-start(f32[1536]{0:T(1024)} %param.15) | copy-start | bytes 18436
Sparse Core Ops, SparseCore 0:
  11.2 124.8 all-gather.7
  139.9 113.0 all-gather.11
  256.7 100.2 all-gather.9
